TPU v7x, 256 devices: a whole 4x4x8 slice. The times are simulated.
256 devices in a mesh: section: 4 (over x), seq: 32 (over z, y), mp: 2 (over core).
Axes of the slice: x: 4, y: 4, z: 8, core: 2. Of those that a mesh axis runs over, the one named last changes fastest.
Arguments:
- text_embed: bfloat16 [320, 8192], P(None, ('seq', 'mp')), may hold values from -6 to 6
- patch_hidden: bfloat16 [256, 5120], P(('section', 'seq', 'mp')), may hold values from -8 to 8
- merge_weight: bfloat16 [5120, 8192], P(None, ('seq', 'mp')), may hold values from -0.078125 to 0.078125
- merge_bias: bfloat16 [8192], P(('seq', 'mp')), may hold values from -3 to 3
- norm_gain: bfloat16 [4, 8192], P('section'), may hold values from 0.5 to 1.5
- query_weight: bfloat16 [4, 8192, 8192], P('section', None, ('seq', 'mp')), may hold values from -0.62285876 to 0.62285876
- key_weight: bfloat16 [4, 8192, 1024], P('section', None, ('seq', 'mp')), may hold values from -0.62285876 to 0.62285876
- value_weight: bfloat16 [4, 8192, 1024], P('section', None, ('seq', 'mp')), may hold values from -0.055242717 to 0.055242717
- image_counts: int32 [2, 4], replicated, may hold values from 1 to 64, 128 in all within a row
- text_counts: int32 [2, 4], replicated, may hold values from 1 to 16, 32 in all within a row
Outputs:
- hidden_states: bfloat16 [4, 320, 8192], P('section', None, ('seq', 'mp'))
Inputs may be any that keep to these rules, and one draw needn't show every extreme that they name: `image_counts`: each micro-batch's image counts sum to 256 / 2. `text_counts`: each micro-batch's image and text counts together sum to 160.
All inputs are finite; a program needn't handle non-finite values.
Results may differ from a plain program's by a relative error of at most 0.017.
Values may be sent and summed in bfloat16 or wider, within the bound.
A program may use at most 64 MiB of HBM per device.

v0:
```python
import math
import jax
import jax.numpy as jnp
from jax import lax
from jax.sharding import PartitionSpec as P

HEADS = 64
HD = 128
KV_HEADS = 8


def from_behind(block, axis, distance):
    devices = range(lax.axis_size(axis))
    route = [(i - distance, i) for i in devices if i - distance in devices]
    return lax.ppermute(block, axis, route)


def layout(image_counts, text_counts, tokens):
    lengths = (image_counts + text_counts).reshape(-1)
    images = image_counts.reshape(-1)
    ends = jnp.cumsum(lengths)
    starts = ends - lengths
    before = jnp.cumsum(images) - images
    position = jnp.arange(tokens, dtype=jnp.int32)
    request = jnp.sum((position[:, None] >= ends[None, :]).astype(jnp.int32), axis=1)
    member = request[:, None] == jnp.arange(lengths.shape[0], dtype=jnp.int32)[None, :]
    first = jnp.sum(jnp.where(member, starts[None, :], 0), axis=1)
    count = jnp.sum(jnp.where(member, images[None, :], 0), axis=1)
    earlier = jnp.sum(jnp.where(member, before[None, :], 0), axis=1)
    offset = position - first
    is_image = (offset >= 1) & (offset <= count)
    row_index = jnp.where(is_image, earlier + offset - 1, 0)
    return (request, is_image, row_index)


def pick_groups(gathered, first_group, local_groups):
    rows_here = gathered.shape[0]
    shaped = gathered.reshape(rows_here, HD, KV_HEADS)
    picked = lax.dynamic_slice_in_dim(shaped, first_group, local_groups, 2)
    return jnp.swapaxes(picked, 1, 2).reshape(rows_here, local_groups * HD)


def shards(
    text_embed,
    patch_hidden,
    merge_weight,
    merge_bias,
    norm_gain,
    query_weight,
    key_weight,
    value_weight,
    image_counts,
    text_counts,
):
    tokens, columns = text_embed.shape
    heads_here = columns // HD
    group_size = HEADS // KV_HEADS
    local_groups = max(1, heads_here // group_size)
    shared_heads = heads_here // local_groups
    first_group = lax.axis_index(("seq", "mp")) * heads_here // group_size
    bias_f = merge_bias.astype(jnp.float32)
    act = jax.nn.gelu(
        lax.all_gather(patch_hidden, ("seq", "mp"), axis=0, tiled=True).astype(jnp.float32),
        approximate=False,
    ).astype(jnp.bfloat16)
    section_rows = (jnp.dot(act, merge_weight, preferred_element_type=jnp.float32) + bias_f).astype(
        jnp.bfloat16
    )
    merged = lax.all_gather(section_rows, "section", axis=0, tiled=True)
    request, is_image, row_index = layout(image_counts, text_counts, tokens)
    start_state = jnp.where(is_image[:, None], jnp.take(merged, row_index, axis=0), text_embed)
    blocks = 2
    rows = tokens // blocks
    depth = lax.axis_size("section")
    section_here = lax.axis_index("section")
    gain = norm_gain[0].astype(jnp.float32)[None, :]
    position = jnp.arange(tokens, dtype=jnp.int32)
    key_cache = jnp.zeros((tokens, local_groups * HD), jnp.bfloat16)
    value_cache = jnp.zeros((tokens, local_groups * HD), jnp.bfloat16)
    hidden = jnp.zeros((tokens, columns), jnp.bfloat16)
    incoming = jnp.zeros((rows, columns), jnp.bfloat16)
    turns = blocks + depth - 1
    for tick in range(turns):
        block = tick - section_here
        valid = (block >= 0) & (block < blocks)
        first_row = jnp.clip(block, 0, blocks - 1) * rows
        if tick < blocks:
            fresh = start_state[tick * rows : (tick + 1) * rows]
            current = jnp.where(section_here == 0, fresh, incoming)
        else:
            current = incoming
        whole = lax.all_gather(current, ("seq", "mp"), axis=1, tiled=True)
        xf = whole.astype(jnp.float32)
        scale = lax.rsqrt(jnp.mean(xf * xf, axis=1, keepdims=True) + 1e-06)
        normed = (xf * scale * gain).astype(jnp.bfloat16)
        query = jnp.dot(normed, query_weight[0], preferred_element_type=jnp.float32).astype(
            jnp.bfloat16
        )
        key_part = jnp.dot(normed, key_weight[0], preferred_element_type=jnp.float32).astype(
            jnp.bfloat16
        )
        value_part = jnp.dot(normed, value_weight[0], preferred_element_type=jnp.float32).astype(
            jnp.bfloat16
        )
        key_all, value_all = (
            lax.all_gather(key_part, ("seq", "mp"), axis=1, tiled=True),
            lax.all_gather(value_part, ("seq", "mp"), axis=1, tiled=True),
        )
        key = pick_groups(key_all, first_group, local_groups)
        value = pick_groups(value_all, first_group, local_groups)
        key_cache = jnp.where(
            valid, lax.dynamic_update_slice_in_dim(key_cache, key, first_row, 0), key_cache
        )
        value_cache = jnp.where(
            valid, lax.dynamic_update_slice_in_dim(value_cache, value, first_row, 0), value_cache
        )
        query_request = lax.dynamic_slice_in_dim(request, first_row, rows)
        query_position = first_row + jnp.arange(rows, dtype=jnp.int32)
        allowed = (request[None, :] == query_request[:, None]) & (
            position[None, :] <= query_position[:, None]
        )
        scores = jnp.einsum(
            "qngd,knd->ngqk",
            query.reshape(rows, local_groups, shared_heads, HD),
            key_cache.reshape(tokens, local_groups, HD),
            preferred_element_type=jnp.float32,
        ) / math.sqrt(HD)
        scores = jnp.where(allowed[None, None, :, :], scores, -1e30)
        probs = jax.nn.softmax(scores, axis=-1).astype(jnp.bfloat16)
        attended = jnp.einsum(
            "ngqk,knd->qngd",
            probs,
            value_cache.reshape(tokens, local_groups, HD),
            preferred_element_type=jnp.float32,
        ).reshape(rows, columns)
        state = (current.astype(jnp.float32) + attended).astype(jnp.bfloat16)
        hidden = jnp.where(
            valid, lax.dynamic_update_slice_in_dim(hidden, state, first_row, 0), hidden
        )
        if tick + 1 < turns:
            incoming = from_behind(state, "section", 1)
    return hidden[None]


def solution(mesh):
    in_specs = (
        P(None, ("seq", "mp")),
        P(("section", "seq", "mp"), None),
        P(None, ("seq", "mp")),
        P(("seq", "mp")),
        P("section", None),
        P("section", None, ("seq", "mp")),
        P("section", None, ("seq", "mp")),
        P("section", None, ("seq", "mp")),
        P(),
        P(),
    )
    out_specs = P("section", None, ("seq", "mp"))
    return jax.shard_map(shards, mesh=mesh, in_specs=in_specs, out_specs=out_specs, check_vma=False)
```

profile of v0, /device:TPU:1, one launch (start us, length us, event | category | flops | bytes accessed | tf_op | source)
XLA Modules:
  0.0 1018.5 jit_solution(12970196134366100098)
XLA Ops:
  9.1 55.3 %all-gather = bf16[64,1,5120]{2,1,0:T(2,128)(2,1)S(1)} all-gather(bf16[1,1,5120]{2,1,0:T(2,128)(2,1)} %bitcast.312), channel_id=1, replica_groups=mesh['section'=4,'seq'=32,'mp'=2] {'seq','mp'}, dimensions={0}, use_global_device_ids=true | all-gather | bytes 665600 | tf_op jit(solution)/shard_map/all_gather | solution.py:63
  68.8 4.7 fusion.80
  73.5 9.6 all_gather.52
  85.6 72.4 %all-gather.7.cloned.1.call-done = bf16[160,8192]{1,0:T(8,128)(2,1)} async-done(((bf16[160,128]{1,0:T(8,128)(2,1)}), bf16[160,8192]{1,0:T(8,128)(2,1)}) %all-gather.7.cloned.1.call-update) | async-done | bytes 2621456 | tf_op jit(solution)/shard_map/all_gather | solution.py:92
  158.0 2.5 fusion
  163.6 50.3 %all_gather.55 = bf16[160,1024]{0,1:T(8,128)(2,1)S(1)} all-gather(bf16[160,16]{0,1:T(8,128)(2,1)S(1)} %convolution_convert_fusion.8), channel_id=1, replica_groups=mesh['section'=4,'seq'=32,'mp'=2] {'seq','mp'}, dimensions={1}, use_global_device_ids=true | all-gather | bytes 332800 | tf_op jit(solution)/shard_map/all_gather | solution.py:106
  214.2 2.5 convolution_convert_fusion.9
  216.7 49.6 %all_gather.54 = bf16[160,1024]{0,1:T(8,128)(2,1)S(1)} all-gather(bf16[160,16]{0,1:T(8,128)(2,1)S(1)} %convolution_convert_fusion.9), channel_id=1, replica_groups=mesh['section'=4,'seq'=32,'mp'=2] {'seq','mp'}, dimensions={1}, use_global_device_ids=true | all-gather | bytes 332800 | tf_op jit(solution)/shard_map/all_gather | solution.py:107
  266.6 2.8 fusion.149
  270.0 3.1 collective-permute-start
  274.9 71.6 %all-gather.9.cloned.1.call-done = bf16[160,8192]{1,0:T(8,128)(2,1)} async-done(((bf16[160,128]{1,0:T(8,128)(2,1)}), bf16[160,8192]{1,0:T(8,128)(2,1)}) %all-gather.9.cloned.1.call-update) | async-done | bytes 2621456 | tf_op jit(solution)/shard_map/all_gather | solution.py:92
  346.5 2.5 fusion.3
  351.4 50.5 %all_gather.57 = bf16[160,1024]{0,1:T(8,128)(2,1)S(1)} all-gather(bf16[160,16]{0,1:T(8,128)(2,1)S(1)} %convolution_convert_fusion.7), channel_id=1, replica_groups=mesh['section'=4,'seq'=32,'mp'=2] {'seq','mp'}, dimensions={1}, use_global_device_ids=true | all-gather | bytes 332800 | tf_op jit(solution)/shard_map/all_gather | solution.py:107
  402.1 49.6 %all_gather.58 = bf16[160,1024]{0,1:T(8,128)(2,1)S(1)} all-gather(bf16[160,16]{0,1:T(8,128)(2,1)S(1)} %convolution_convert_fusion.6), channel_id=1, replica_groups=mesh['section'=4,'seq'=32,'mp'=2] {'seq','mp'}, dimensions={1}, use_global_device_ids=true | all-gather | bytes 332800 | tf_op jit(solution)/shard_map/all_gather | solution.py:106
  452.1 2.8 fusion.152
  455.4 3.1 collective-permute-start.1
  460.3 71.6 %all-gather.11.cloned.1.call-done = bf16[160,8192]{1,0:T(8,128)(2,1)} async-done(((bf16[160,128]{1,0:T(8,128)(2,1)}), bf16[160,8192]{1,0:T(8,128)(2,1)}) %all-gather.11.cloned.1.call-update) | async-done | bytes 2621456 | tf_op jit(solution)/shard_map/all_gather | solution.py:92
  536.7 50.3 %all_gather.61 = bf16[160,1024]{0,1:T(8,128)(2,1)S(1)} all-gather(bf16[160,16]{0,1:T(8,128)(2,1)S(1)} %convolution_convert_fusion.4), channel_id=1, replica_groups=mesh['section'=4,'seq'=32,'mp'=2] {'seq','mp'}, dimensions={1}, use_global_device_ids=true | all-gather | bytes 332800 | tf_op jit(solution)/shard_map/all_gather | solution.py:106
  587.3 49.6 %all_gather.60 = bf16[160,1024]{0,1:T(8,128)(2,1)S(1)} all-gather(bf16[160,16]{0,1:T(8,128)(2,1)S(1)} %convolution_convert_fusion.5), channel_id=1, replica_groups=mesh['section'=4,'seq'=32,'mp'=2] {'seq','mp'}, dimensions={1}, use_global_device_ids=true | all-gather | bytes 332800 | tf_op jit(solution)/shard_map/all_gather | solution.py:107
  637.2 2.8 fusion.155
  640.6 3.1 collective-permute-start.2
  645.5 71.6 %all-gather.13.cloned.1.call-done = bf16[160,8192]{1,0:T(8,128)(2,1)} async-done(((bf16[160,128]{1,0:T(8,128)(2,1)}), bf16[160,8192]{1,0:T(8,128)(2,1)}) %all-gather.13.cloned.1.call-update) | async-done | bytes 2621456 | tf_op jit(solution)/shard_map/all_gather | solution.py:92
  717.0 2.5 fusion.9
  721.9 50.3 %all_gather.64 = bf16[160,1024]{0,1:T(8,128)(2,1)S(1)} all-gather(bf16[160,16]{0,1:T(8,128)(2,1)S(1)} %convolution_convert_fusion.2), channel_id=1, replica_groups=mesh['section'=4,'seq'=32,'mp'=2] {'seq','mp'}, dimensions={1}, use_global_device_ids=true | all-gather | bytes 332800 | tf_op jit(solution)/shard_map/all_gather | solution.py:106
  772.5 49.6 %all_gather.63 = bf16[160,1024]{0,1:T(8,128)(2,1)S(1)} all-gather(bf16[160,16]{0,1:T(8,128)(2,1)S(1)} %convolution_convert_fusion.3), channel_id=1, replica_groups=mesh['section'=4,'seq'=32,'mp'=2] {'seq','mp'}, dimensions={1}, use_global_device_ids=true | all-gather | bytes 332800 | tf_op jit(solution)/shard_map/all_gather | solution.py:107
  822.4 2.8 fusion.158
  825.8 3.1 collective-permute-start.3
  831.2 71.0 %all-gather.15.cloned.1.call-done = bf16[160,8192]{1,0:T(8,128)(2,1)} async-done(((bf16[160,128]{1,0:T(8,128)(2,1)}), bf16[160,8192]{1,0:T(8,128)(2,1)}) %all-gather.15.cloned.1.call-update) | async-done | bytes 2621456 | tf_op jit(solution)/shard_map/all_gather | solution.py:92
  902.2 2.5 fusion.12
  907.1 50.1 %all_gather.67 = bf16[160,1024]{0,1:T(8,128)(2,1)S(1)} all-gather(bf16[160,16]{0,1:T(8,128)(2,1)S(1)} %convolution_convert_fusion), channel_id=1, replica_groups=mesh['section'=4,'seq'=32,'mp'=2] {'seq','mp'}, dimensions={1}, use_global_device_ids=true | all-gather | bytes 332800 | tf_op jit(solution)/shard_map/all_gather | solution.py:106
  957.4 49.9 %all_gather.66 = bf16[160,1024]{0,1:T(8,128)(2,1)S(1)} all-gather(bf16[160,16]{0,1:T(8,128)(2,1)S(1)} %convolution_convert_fusion.1), channel_id=1, replica_groups=mesh['section'=4,'seq'=32,'mp'=2] {'seq','mp'}, dimensions={1}, use_global_device_ids=true | all-gather | bytes 332800 | tf_op jit(solution)/shard_map/all_gather | solution.py:107
  1007.6 2.8 fusion.161
  (153 shorter events, 37.7 us)
Async XLA Ops:
  6.5 260.1 %copy-start = (bf16[1,8192,128]{2,1,0:T(8,128)(2,1)S(1)}, bf16[1,8192,128]{2,1,0:T(8,128)(2,1)}, u32[]{:S(2)}) copy-start(bf16[1,8192,128]{2,1,0:T(8,128)(2,1)} %param.15) | copy-start | bytes 6291460
  6.5 151.5 %all-gather.7.cloned.1.call-start = ((), (), s32[]{:S(2)}) async-start(), calls=%async_computation | async-start | bytes 2662400 | tf_op jit(solution)/shard_map/all_gather | solution.py:92
  64.3 4.4 copy-start.23
  68.8 15.8 %copy-start.15 = (bf16[320,128]{1,0:T(8,128)(2,1)S(1)}, bf16[320,128]{1,0:T(8,128)(2,1)}, u32[]{:S(2)}) copy-start(bf16[320,128]{1,0:T(8,128)(2,1)} %param.10) | copy-start | bytes 245764
  68.8 16.7 %copy-start.22 = (bf16[1,8192]{1,0:T(2,128)(2,1)S(1)}, bf16[1,8192]{1,0:T(2,128)(2,1)}, u32[]{:S(2)}) copy-start(bf16[1,8192]{1,0:T(2,128)(2,1)} %param.14) | copy-start | bytes 49156
  85.4 261.2 %all-gather.9.cloned.1.call-start = ((), (), s32[]{:S(2)}) async-start(), calls=%async_computation.1 | async-start | bytes 2662400 | tf_op jit(solution)/shard_map/all_gather | solution.py:92
  158.0 2.5 copy-start.6
  160.6 2.2 copy-start.11
  161.3 1.5 copy-start.5
  162.8 51.4 %copy-start.12 = (bf16[1,8192,16]{1,2,0:T(8,128)(2,1)S(1)}, bf16[1,8192,16]{1,2,0:T(8,128)(2,1)}, u32[]{:S(2)}) copy-start(bf16[1,8192,16]{1,2,0:T(8,128)(2,1)} %param.17) | copy-start | bytes 786436
  266.6 3.1 copy-start.13
  270.0 4.2 collective-permute-start
  274.9 257.0 %all-gather.11.cloned.1.call-start = ((), (), s32[]{:S(2)}) async-start(), calls=%async_computation.2 | async-start | bytes 2662400 | tf_op jit(solution)/shard_map/all_gather | solution.py:92
  346.5 2.5 copy-start.8
  349.8 1.6 copy-start.2
  452.1 3.1 copy-start.14
  455.4 4.2 collective-permute-start.1
  459.6 0.6 copy-start.18
  460.2 256.8 %all-gather.13.cloned.1.call-start = ((), (), s32[]{:S(2)}) async-start(), calls=%async_computation.3 | async-start | bytes 2662400 | tf_op jit(solution)/shard_map/all_gather | solution.py:92
  531.9 2.5 copy-start.9
  535.1 1.6 copy-start.3
  637.2 3.1 copy-start.19
  640.6 4.2 collective-permute-start.2
  644.8 0.6 copy-start.20
  645.4 256.8 %all-gather.15.cloned.1.call-start = ((), (), s32[]{:S(2)}) async-start(), calls=%async_computation.4 | async-start | bytes 2662400 | tf_op jit(solution)/shard_map/all_gather | solution.py:92
  717.0 2.5 copy-start.10
  720.3 1.6 copy-start.4
  822.4 3.1 copy-start.21
  825.8 4.2 collective-permute-start.3
  902.2 2.5 copy-start.7
  905.5 1.6 copy-start.1
  1007.6 3.1 copy-start.17
  (1 other events, 0.6 us)
Sparse Core Ops, SparseCore 0:
  85.5 72.5 all-gather.6
  275.0 71.4 all-gather.8
  460.4 71.4 all-gather.10
  645.5 71.4 all-gather.12
  830.7 71.4 all-gather.14
where the time goes:
time: 1030 us; the launch traced here: 1020 us
  blocking collectives  565 us (55%)
  waiting for transfers between devices  363 us (35%)
  matrix products  30.4 us (3%)
  other arithmetic  24.1 us (2%)
  between operations  14.2 us (1%)
  starting transfers between devices  12.5 us (1%)
    all_gather x5, waiting for transfers between devices, shards(): whole = lax.all_gather(current, ('seq', 'mp'), axis=1, tiled=True)  358 us
    all_gather x5, blocking collectives, shards(): lax.all_gather(key_part, ('seq', 'mp'), axis=1, tiled=True)  251 us
    all_gather x5, blocking collectives, shards(): lax.all_gather(value_part, ('seq', 'mp'), axis=1, tiled=True)  249 us
    all_gather x1, blocking collectives, shards(): lax.all_gather(patch_hidden, ('seq', 'mp'), axis=0, tiled=True)  55.3 us
  transfers between devices with their start and end apart: 9, of which 9 were waited for; matrix products, arithmetic and copies ran while one was open for 0% of the time, Pallas kernels for 0%

commit v1 on v0

--- a/solution.py
+++ b/solution.py
@@ -104,7 +104,12 @@
         )
         key_all, value_all = (
             lax.all_gather(key_part, ("seq", "mp"), axis=1, tiled=True),
-            lax.all_gather(value_part, ("seq", "mp"), axis=1, tiled=True),
+            jnp.concatenate(
+                lax.all_to_all(
+                    jnp.stack([value_part] * lax.axis_size(("seq", "mp"))), ("seq", "mp"), 0, 0
+                ),
+                axis=1,
+            ),
         )
         key = pick_groups(key_all, first_group, local_groups)
         value = pick_groups(value_all, first_group, local_groups)

time: 1030 us -> 903 us (0.88)
  blocking collectives: 565 us -> 320 us
  waiting for transfers between devices: 363 us -> 419 us
  starting transfers between devices: 12.5 us -> 48.9 us
  local copies, waits for them, and re-layouts: 10 us -> 23.2 us
    all_gather x5 -> x0, blocking collectives: 249 us -> none  [shards(): lax.all_gather(value_part, ('seq', 'mp'), axis=1, tiled=True)]
    all_to_all x0 -> x5, waiting for transfers between devices: none -> 55.9 us  [shards(): lax.all_to_all(jnp.stack([value_part] * lax.axis_size(('seq', 'mp'))), ('...]
    all_to_all x0 -> x5, starting transfers between devices: none -> 35.8 us  [shards(): lax.all_to_all(jnp.stack([value_part] * lax.axis_size(('seq', 'mp'))), ('...]
  transfers between devices with their start and end apart: 9 -> 14, of which waited for: 9 -> 13; matrix products, arithmetic and copies ran while one was open for 0% -> 2% of each run, Pallas kernels for 0% -> 0%
where the time goes in v1:
time: 903 us; the launch traced here: 893 us
  waiting for transfers between devices  419 us (46%)
  blocking collectives  320 us (35%)
  starting transfers between devices  48.9 us (5%)
  matrix products  36 us (4%)
  other arithmetic  31.9 us (4%)
  local copies, waits for them, and re-layouts  23.2 us (3%)
  between operations  14.1 us (2%)
    all_gather x5, waiting for transfers between devices, shards(): whole = lax.all_gather(current, ('seq', 'mp'), axis=1, tiled=True)  359 us
    all_gather x5, blocking collectives, shards(): lax.all_gather(key_part, ('seq', 'mp'), axis=1, tiled=True)  255 us
    all_to_all x5, waiting for transfers between devices, shards(): lax.all_to_all(jnp.stack([value_part] * lax.axis_size(('seq', 'mp'))), ('...  55.9 us
    all_gather x1, blocking collectives, shards(): lax.all_gather(patch_hidden, ('seq', 'mp'), axis=0, tiled=True)  55.3 us
    all_to_all x5, starting transfers between devices, shards(): lax.all_to_all(jnp.stack([value_part] * lax.axis_size(('seq', 'mp'))), ('...  35.8 us
  transfers between devices with their start and end apart: 14, of which 13 were waited for; matrix products, arithmetic and copies ran while one was open for 2% of the time, Pallas kernels for 0%

profile of v1, /device:TPU:1, one launch (start us, length us, event | category | flops | bytes accessed | tf_op | source)
XLA Modules:
  0.0 892.8 jit_solution(811815168625584687)
XLA Ops:
  9.1 55.3 %all-gather = bf16[64,1,5120]{2,1,0:T(2,128)(2,1)S(1)} all-gather(bf16[1,1,5120]{2,1,0:T(2,128)(2,1)} %bitcast.322), channel_id=1, replica_groups=mesh['section'=4,'seq'=32,'mp'=2] {'seq','mp'}, dimensions={0}, use_global_device_ids=true | all-gather | bytes 665600 | tf_op jit(solution)/shard_map/all_gather | solution.py:63
  68.8 4.7 fusion.80
  73.5 9.6 %all_gather.37 = bf16[256,128]{1,0:T(8,128)(2,1)S(1)} all-gather(bf16[64,128]{1,0:T(8,128)(2,1)S(1)} %fusion.80), channel_id=1, replica_groups=mesh['section'=4,'seq'=32,'mp'=2] {'section'}, dimensions={0}, use_global_device_ids=true | all-gather | bytes 81920 | tf_op jit(solution)/shard_map/all_gather | solution.py:69
  86.8 71.9 %all-gather.7.cloned.1.call-done = bf16[160,8192]{1,0:T(8,128)(2,1)} async-done(((bf16[160,128]{1,0:T(8,128)(2,1)}), bf16[160,8192]{1,0:T(8,128)(2,1)}) %all-gather.7.cloned.1.call-update) | async-done | bytes 2621456 | tf_op jit(solution)/shard_map/all_gather | solution.py:92
  164.2 50.3 %all_gather.39 = bf16[160,1024]{0,1:T(8,128)(2,1)S(1)} all-gather(bf16[160,16]{0,1:T(8,128)(2,1)S(1)} %convolution_convert_fusion.8), channel_id=1, replica_groups=mesh['section'=4,'seq'=32,'mp'=2] {'seq','mp'}, dimensions={1}, use_global_device_ids=true | all-gather | bytes 332800 | tf_op jit(solution)/shard_map/all_gather | solution.py:106
  214.8 2.5 convolution_convert_fusion.9
  218.2 6.9 all-to-all-start
  225.2 2.8 fusion.149
  228.9 13.9 %all-to-all-done = bf16[64,160,16]{1,2,0:T(8,128)(2,1)S(1)} async-done(((bf16[64,160,16]{1,2,0:T(8,128)(2,1)}), bf16[64,160,16]{1,2,0:T(8,128)(2,1)S(1)}, u32[]{:S(2)}, u32[]{:S(2)}) %all-to-all-start) | async-done | bytes 327712 | tf_op jit(solution)/shard_map/all_to_all | solution.py:108
  245.8 3.1 collective-permute-start
  251.4 71.6 %all-gather.9.cloned.1.call-done = bf16[160,8192]{1,0:T(8,128)(2,1)} async-done(((bf16[160,128]{1,0:T(8,128)(2,1)}), bf16[160,8192]{1,0:T(8,128)(2,1)}) %all-gather.9.cloned.1.call-update) | async-done | bytes 2621456 | tf_op jit(solution)/shard_map/all_gather | solution.py:92
  329.4 8.0 all-to-all-start.1
  340.6 54.5 %all_gather.41 = bf16[160,1024]{0,1:T(8,128)(2,1)S(1)} all-gather(bf16[160,16]{0,1:T(8,128)(2,1)S(1)} %convolution_convert_fusion.6), channel_id=1, replica_groups=mesh['section'=4,'seq'=32,'mp'=2] {'seq','mp'}, dimensions={1}, use_global_device_ids=true | all-gather | bytes 332800 | tf_op jit(solution)/shard_map/all_gather | solution.py:106
  397.1 2.9 fusion.152
  400.5 3.1 collective-permute-start.1
  405.9 74.2 %all-gather.11.cloned.1.call-done = bf16[160,8192]{1,0:T(8,128)(2,1)} async-done(((bf16[160,128]{1,0:T(8,128)(2,1)}), bf16[160,8192]{1,0:T(8,128)(2,1)}) %all-gather.11.cloned.1.call-update) | async-done | bytes 2621456 | tf_op jit(solution)/shard_map/all_gather | solution.py:92
  484.9 50.1 %all_gather.43 = bf16[160,1024]{0,1:T(8,128)(2,1)S(1)} all-gather(bf16[160,16]{0,1:T(8,128)(2,1)S(1)} %convolution_convert_fusion.4), channel_id=1, replica_groups=mesh['section'=4,'seq'=32,'mp'=2] {'seq','mp'}, dimensions={1}, use_global_device_ids=true | all-gather | bytes 332800 | tf_op jit(solution)/shard_map/all_gather | solution.py:106
  536.1 6.9 all-to-all-start.2
  543.5 2.8 fusion.155
  547.2 13.5 %all-to-all-done.2 = bf16[64,160,16]{1,2,0:T(8,128)(2,1)S(1)} async-done(((bf16[64,160,16]{1,2,0:T(8,128)(2,1)}), bf16[64,160,16]{1,2,0:T(8,128)(2,1)S(1)}, u32[]{:S(2)}, u32[]{:S(2)}) %all-to-all-start.2) | async-done | bytes 327712 | tf_op jit(solution)/shard_map/all_to_all | solution.py:108
  565.7 3.1 collective-permute-start.2
  571.1 71.0 %all-gather.13.cloned.1.call-done = bf16[160,8192]{1,0:T(8,128)(2,1)} async-done(((bf16[160,128]{1,0:T(8,128)(2,1)}), bf16[160,8192]{1,0:T(8,128)(2,1)}) %all-gather.13.cloned.1.call-update) | async-done | bytes 2621456 | tf_op jit(solution)/shard_map/all_gather | solution.py:92
  646.9 50.1 %all_gather.45 = bf16[160,1024]{0,1:T(8,128)(2,1)S(1)} all-gather(bf16[160,16]{0,1:T(8,128)(2,1)S(1)} %convolution_convert_fusion.2), channel_id=1, replica_groups=mesh['section'=4,'seq'=32,'mp'=2] {'seq','mp'}, dimensions={1}, use_global_device_ids=true | all-gather | bytes 332800 | tf_op jit(solution)/shard_map/all_gather | solution.py:106
  698.2 6.9 all-to-all-start.3
  705.2 2.8 fusion.158
  708.8 14.0 %all-to-all-done.3 = bf16[64,160,16]{1,2,0:T(8,128)(2,1)S(1)} async-done(((bf16[64,160,16]{1,2,0:T(8,128)(2,1)}), bf16[64,160,16]{1,2,0:T(8,128)(2,1)S(1)}, u32[]{:S(2)}, u32[]{:S(2)}) %all-to-all-start.3) | async-done | bytes 327712 | tf_op jit(solution)/shard_map/all_to_all | solution.py:108
  727.8 3.3 collective-permute-start.3
  734.1 70.0 %all-gather.15.cloned.1.call-done = bf16[160,8192]{1,0:T(8,128)(2,1)} async-done(((bf16[160,128]{1,0:T(8,128)(2,1)}), bf16[160,8192]{1,0:T(8,128)(2,1)}) %all-gather.15.cloned.1.call-update) | async-done | bytes 2621456 | tf_op jit(solution)/shard_map/all_gather | solution.py:92
  809.0 50.1 %all_gather.47 = bf16[160,1024]{0,1:T(8,128)(2,1)S(1)} all-gather(bf16[160,16]{0,1:T(8,128)(2,1)S(1)} %convolution_convert_fusion), channel_id=1, replica_groups=mesh['section'=4,'seq'=32,'mp'=2] {'seq','mp'}, dimensions={1}, use_global_device_ids=true | all-gather | bytes 332800 | tf_op jit(solution)/shard_map/all_gather | solution.py:106
  860.2 6.9 all-to-all-start.4
  867.2 2.9 fusion.161
  870.3 14.5 %all-to-all-done.4 = bf16[64,160,16]{1,2,0:T(8,128)(2,1)S(1)} async-done(((bf16[64,160,16]{1,2,0:T(8,128)(2,1)}), bf16[64,160,16]{1,2,0:T(8,128)(2,1)S(1)}, u32[]{:S(2)}, u32[]{:S(2)}) %all-to-all-start.4) | async-done | bytes 327712 | tf_op jit(solution)/shard_map/all_to_all | solution.py:108
  (179 shorter events, 74.4 us)
Async XLA Ops:
  6.5 218.7 %copy-start = (bf16[1,8192,128]{2,1,0:T(8,128)(2,1)S(1)}, bf16[1,8192,128]{2,1,0:T(8,128)(2,1)}, u32[]{:S(2)}) copy-start(bf16[1,8192,128]{2,1,0:T(8,128)(2,1)} %param.15) | copy-start | bytes 6291460
  6.5 152.2 %all-gather.7.cloned.1.call-start = ((), (), s32[]{:S(2)}) async-start(), calls=%async_computation.5 | async-start | bytes 2662400 | tf_op jit(solution)/shard_map/all_gather | solution.py:92
  64.3 4.4 copy-start.31
  68.4 156.8 %copy-start.18 = (s32[320]{0:T(512)}, s32[320]{0:T(512)S(1)}, u32[]{:S(2)}) copy-start(s32[320]{0:T(512)S(1)} %convert_reduce_fusion) | copy-start | bytes 3844
  68.8 15.8 %copy-start.21 = (bf16[320,128]{1,0:T(8,128)(2,1)S(1)}, bf16[320,128]{1,0:T(8,128)(2,1)}, u32[]{:S(2)}) copy-start(bf16[320,128]{1,0:T(8,128)(2,1)} %param.10) | copy-start | bytes 245764
  68.8 17.3 %copy-start.28 = (bf16[1,8192]{1,0:T(2,128)(2,1)S(1)}, bf16[1,8192]{1,0:T(2,128)(2,1)}, u32[]{:S(2)}) copy-start(bf16[1,8192]{1,0:T(2,128)(2,1)} %param.14) | copy-start | bytes 49156
  158.7 2.5 copy-start.6
  163.5 51.3 %copy-start.12 = (bf16[1,8192,16]{1,2,0:T(8,128)(2,1)S(1)}, bf16[1,8192,16]{1,2,0:T(8,128)(2,1)}, u32[]{:S(2)}) copy-start(bf16[1,8192,16]{1,2,0:T(8,128)(2,1)} %param.17) | copy-start | bytes 786436
  218.2 24.6 %all-to-all-start = ((bf16[64,160,16]{1,2,0:T(8,128)(2,1)}), bf16[64,160,16]{1,2,0:T(8,128)(2,1)S(1)}, u32[]{:S(2)}, u32[]{:S(2)}) async-start(bf16[64,160,16]{1,2,0:T(8,128)(2,1)} %stack.10), calls=%async_computation | async-start | bytes 1048576 | tf_op jit(solution)/shard_map/all_to_all | solution.py:108
  225.1 97.8 %all-gather.9.cloned.1.call-start = ((), (), s32[]{:S(2)}) async-start(), calls=%async_computation.6 | async-start | bytes 2662400 | tf_op jit(solution)/shard_map/all_gather | solution.py:92
  228.1 16.6 %copy-start.29 = (f32[160]{0:T(256)}, f32[160]{0:T(256)S(1)}, u32[]{:S(2)}) copy-start(f32[160]{0:T(256)S(1)} %get-tuple-element.21) | copy-start | bytes 1924
  245.8 4.2 collective-permute-start
  329.4 66.6 %all-to-all-start.1 = ((bf16[64,160,16]{1,2,0:T(8,128)(2,1)}), bf16[64,160,16]{1,2,0:T(8,128)(2,1)S(1)}, u32[]{:S(2)}, u32[]{:S(2)}) async-start(bf16[64,160,16]{1,2,0:T(8,128)(2,1)} %stack.11), calls=%async_computation.1 | async-start | bytes 1048576 | tf_op jit(solution)/shard_map/all_to_all | solution.py:108
  337.4 142.6 %all-gather.11.cloned.1.call-start = ((), (), s32[]{:S(2)}) async-start(), calls=%async_computation.7 | async-start | bytes 2662400 | tf_op jit(solution)/shard_map/all_gather | solution.py:92
  397.1 3.1 copy-start.13
  397.1 3.1 copy-start.20
  400.5 82.8 %copy-start.15 = (bf16[320,128]{1,0:T(8,128)(2,1)}, bf16[320,128]{1,0:T(8,128)(2,1)S(1)}, u32[]{:S(2)}) copy-start(bf16[320,128]{1,0:T(8,128)(2,1)S(1)} %get-tuple-element.12) | copy-start | bytes 245764
  400.5 4.2 collective-permute-start.1
  484.1 59.4 %copy-start.19 = (s32[320]{0:T(512)S(1)}, s32[320]{0:T(512)}, u32[]{:S(2)}) copy-start(s32[320]{0:T(512)} %copy-done.18) | copy-start | bytes 3844
  536.1 24.6 %all-to-all-start.2 = ((bf16[64,160,16]{1,2,0:T(8,128)(2,1)}), bf16[64,160,16]{1,2,0:T(8,128)(2,1)S(1)}, u32[]{:S(2)}, u32[]{:S(2)}) async-start(bf16[64,160,16]{1,2,0:T(8,128)(2,1)} %stack.12), calls=%async_computation.2 | async-start | bytes 1048576 | tf_op jit(solution)/shard_map/all_to_all | solution.py:108
  543.0 99.1 %all-gather.13.cloned.1.call-start = ((), (), s32[]{:S(2)}) async-start(), calls=%async_computation.8 | async-start | bytes 2662400 | tf_op jit(solution)/shard_map/all_gather | solution.py:92
  543.5 20.4 %copy-start.25 = (bf16[160,128]{1,0:T(8,128)(2,1)S(1)}, bf16[160,128]{1,0:T(8,128)(2,1)}, u32[]{:S(2)}) copy-start(bf16[160,128]{1,0:T(8,128)(2,1)} %copy-done.24) | copy-start | bytes 122884
  565.7 4.2 collective-permute-start.2
  698.2 24.6 %all-to-all-start.3 = ((bf16[64,160,16]{1,2,0:T(8,128)(2,1)}), bf16[64,160,16]{1,2,0:T(8,128)(2,1)S(1)}, u32[]{:S(2)}, u32[]{:S(2)}) async-start(bf16[64,160,16]{1,2,0:T(8,128)(2,1)} %stack.13), calls=%async_computation.3 | async-start | bytes 1048576 | tf_op jit(solution)/shard_map/all_to_all | solution.py:108
  705.1 99.1 %all-gather.15.cloned.1.call-start = ((), (), s32[]{:S(2)}) async-start(), calls=%async_computation.9 | async-start | bytes 2662400 | tf_op jit(solution)/shard_map/all_gather | solution.py:92
  705.2 20.8 %copy-start.27 = (bf16[160,128]{1,0:T(8,128)(2,1)S(1)}, bf16[160,128]{1,0:T(8,128)(2,1)}, u32[]{:S(2)}) copy-start(bf16[160,128]{1,0:T(8,128)(2,1)} %copy-done.26) | copy-start | bytes 122884
  727.8 4.2 collective-permute-start.3
  808.2 59.0 %copy-start.30 = (s32[160]{0:T(256)S(1)}, s32[160]{0:T(256)}, u32[]{:S(2)}) copy-start(s32[160]{0:T(256)} %get-tuple-element.16) | copy-start | bytes 1924
  860.2 24.6 %all-to-all-start.4 = ((bf16[64,160,16]{1,2,0:T(8,128)(2,1)}), bf16[64,160,16]{1,2,0:T(8,128)(2,1)S(1)}, u32[]{:S(2)}, u32[]{:S(2)}) async-start(bf16[64,160,16]{1,2,0:T(8,128)(2,1)} %stack.14), calls=%async_computation.4 | async-start | bytes 1048576 | tf_op jit(solution)/shard_map/all_to_all | solution.py:108
  867.2 17.9 %copy-start.14 = (bf16[320,128]{1,0:T(8,128)(2,1)S(1)}, bf16[320,128]{1,0:T(8,128)(2,1)}, u32[]{:S(2)}) copy-start(bf16[320,128]{1,0:T(8,128)(2,1)} %fusion.113) | copy-start | bytes 245764
  867.2 18.0 %copy-start.16 = (bf16[320,128]{1,0:T(8,128)(2,1)S(1)}, bf16[320,128]{1,0:T(8,128)(2,1)}, u32[]{:S(2)}) copy-start(bf16[320,128]{1,0:T(8,128)(2,1)} %get-tuple-element.8) | copy-start | bytes 245764
  867.2 18.0 %copy-start.23 = (bf16[160,128]{1,0:T(8,128)(2,1)S(1)}, bf16[160,128]{1,0:T(8,128)(2,1)}, u32[]{:S(2)}) copy-start(bf16[160,128]{1,0:T(8,128)(2,1)} %copy-done.22) | copy-start | bytes 122884
  (14 other events, 22.7 us)
Sparse Core Ops, SparseCore 0:
  86.1 72.5 all-gather.6
  251.5 71.4 all-gather.8
  405.4 74.5 all-gather.10
  570.6 71.4 all-gather.12
  732.7 71.4 all-gather.14
